TPU v7x, 512 devices: a whole 4x8x8 slice. The times are simulated.
512 devices in a mesh: prow: 32 (over y, x), pcol: 16 (over z, core).
Axes of the slice: x: 4, y: 8, z: 8, core: 2. Of those that a mesh axis runs over, the one named last changes fastest.
Arguments:
- matrix: bfloat16 [4, 8192, 4, 4096], P(None, 'prow', None, 'pcol'), may hold values from -6 to 6
- pivots: int32 [2, 256], replicated, may hold values from 0 to 32767, as said below
- lower_inverse: bfloat16 [2, 256, 256], replicated, as said below
- upper_inverse: bfloat16 [2, 256, 256], replicated, as said below
Outputs:
- factored: bfloat16 [4, 8192, 4, 4096], P(None, 'prow', None, 'pcol')
Inputs may be any that keep to these rules, and one draw needn't show every extreme that they name: For each panel k and each i, pivots[k, i] is either k * 256 + i or a row at or after (k + 1) * 256; entry 0 of each list is k * 256; the rows of one panel's list are distinct, and each list names row 32767. Each lower_inverse[k] is unit lower triangular. Each upper_inverse[k] is upper triangular with positive diagonal.
All inputs are finite; a program needn't handle non-finite values.
Results may differ from a plain program's by a relative error of at most 0.0079.
Values may be sent and summed in bfloat16 or wider, within the bound.
A program may use at most 64 MiB of HBM per device.

v0:
```python
import jax
import jax.numpy as jnp
from jax import lax
from jax.sharding import PartitionSpec as P


def spread(block, axis, source):
    block = jnp.where(lax.axis_index(axis) == source, block, jnp.zeros_like(block))
    return lax.psum(block, axis)


def local(matrix, pivots, lower_inverse, upper_inverse):
    row_count = lax.axis_size("prow")
    col_count = lax.axis_size("pcol")
    my_row = lax.axis_index("prow")
    my_col = lax.axis_index("pcol")
    blocks_down, block, blocks_across, _ = matrix.shape
    local_rows = blocks_down * block
    local_cols = blocks_across * block
    current = matrix.reshape(local_rows, local_cols)
    row_place = jnp.arange(local_rows)
    col_place = jnp.arange(local_cols)
    global_rows = (row_place // block * row_count + my_row) * block + row_place % block
    global_cols = (col_place // block * col_count + my_col) * block + col_place % block
    for panel in range(pivots.shape[0]):
        start = panel * block
        chosen = pivots[panel]
        block_row = chosen // block
        is_mine = block_row % row_count == my_row
        local_index = block_row // row_count * block + chosen % block
        safe_index = jnp.where(is_mine, local_index, 0)
        picked = jnp.where(is_mine[:, None], current[safe_index], jnp.zeros((), jnp.bfloat16))
        top_holder = panel % row_count
        top_first = panel // row_count * block
        is_top = my_row == top_holder
        top_local = current[top_first : top_first + block]
        incoming = lax.psum(picked, "prow").astype(jnp.float32)
        old_top = spread(top_local, "prow", top_holder)
        incoming = incoming.astype(jnp.bfloat16)
        target = jnp.where(is_mine, local_index, local_rows)
        current = current.at[target].set(old_top, mode="drop")
        top_now = current[top_first : top_first + block]
        current = current.at[top_first : top_first + block].set(
            jnp.where(is_top, incoming, top_now)
        )
        panel_holder = panel % col_count
        panel_first = panel // col_count * block
        panel_cols = current[:, panel_first : panel_first + block]
        factor = jnp.dot(
            panel_cols, upper_inverse[panel], preferred_element_type=jnp.float32
        ).astype(jnp.bfloat16)
        lower = spread(factor, "pcol", panel_holder)
        top_rows_now = current[top_first : top_first + block]
        upper_local = jnp.dot(
            lower_inverse[panel], top_rows_now, preferred_element_type=jnp.float32
        ).astype(jnp.bfloat16)
        upper = spread(upper_local, "prow", top_holder)
        row_mask = global_rows >= start + block
        col_mask = global_cols >= start + block
        product = jnp.dot(lower, upper, preferred_element_type=jnp.float32)
        changed = (current.astype(jnp.float32) - product).astype(jnp.bfloat16)
        current = jnp.where(row_mask[:, None] & col_mask[None, :], changed, current)
        panel_now = current[:, panel_first : panel_first + block]
        is_panel = my_col == panel_holder
        current = current.at[:, panel_first : panel_first + block].set(
            jnp.where(is_panel & row_mask[:, None], lower, panel_now)
        )
        top_now = current[top_first : top_first + block]
        current = current.at[top_first : top_first + block].set(
            jnp.where(is_top & col_mask[None, :], upper, top_now)
        )
    return current.reshape(matrix.shape)


def solution(mesh):
    in_specs = (P(None, "prow", None, "pcol"), P(), P(), P())
    out_specs = P(None, "prow", None, "pcol")
    return jax.shard_map(local, mesh=mesh, in_specs=in_specs, out_specs=out_specs, check_vma=False)
```

profile of v0, /device:TPU:64, one launch (start us, length us, event | category | flops | bytes accessed | tf_op | source)
XLA Modules:
  0.0 935.4 jit_solution(9245979962297047601)
XLA Ops:
  6.5 0.8 and_select_fusion.5
  7.3 0.8 fusion.48
  8.1 2.1 copy.23
  10.2 1.3 slice_select_fusion.4
  11.5 0.9 copy.24
  12.4 1.2 gather_fusion
  13.5 0.9 broadcast_select_fusion.1
  14.6 164.6 %all-reduce.19.cloned.1.call-done = (bf16[256,1024]{1,0:T(8,128)(2,1)}, bf16[256,1024]{1,0:T(8,128)(2,1)}) async-done(((bf16[256,1024]{1,0:T(8,128)(2,1)}, bf16[256,1024]{1,0:T(8,128)(2,1)}), (bf16[256,1024]{1,0:T(8,128)(2,1)}, bf16[256,1024]{1,0:T(8,128)(2,1)})) %all-reduce.19.cloned.1.call-update) | async-done | bytes 1048592 | tf_op jit(solution)/shard_map/psum | solution.py:9
  179.2 3.3 scatter_fusion
  182.6 1.1 fusion.3
  183.9 1.1 fusion
  185.1 0.7 compare_reduce_fusion
  185.9 109.8 %all-reduce.9.cloned.1.call-done = bf16[1024,256]{1,0:T(8,128)(2,1)} async-done(((bf16[1024,256]{1,0:T(8,128)(2,1)}), bf16[1024,256]{1,0:T(8,128)(2,1)}) %all-reduce.9.cloned.1.call-update) | async-done | bytes 524304 | tf_op jit(solution)/shard_map/psum | solution.py:9
  295.8 164.5 %all-reduce.11.cloned.1.call-done = bf16[256,1024]{1,0:T(8,128)(2,1)} async-done(((bf16[256,1024]{1,0:T(8,128)(2,1)}), bf16[256,1024]{1,0:T(8,128)(2,1)}) %all-reduce.11.cloned.1.call-update) | async-done | bytes 524304 | tf_op jit(solution)/shard_map/psum | solution.py:9
  460.3 3.6 and_select_fusion
  463.8 2.9 fusion.6
  466.8 2.3 broadcast_select_fusion.2
  469.1 3.4 gather_fusion.1
  472.5 0.9 broadcast_select_fusion
  473.5 158.0 %all-reduce.17.cloned.1.call-done = (bf16[256,1024]{1,0:T(8,128)(2,1)}, bf16[256,1024]{1,0:T(8,128)(2,1)}) async-done(((bf16[256,1024]{1,0:T(8,128)(2,1)}, bf16[256,1024]{1,0:T(8,128)(2,1)}), (bf16[256,1024]{1,0:T(8,128)(2,1)}, bf16[256,1024]{1,0:T(8,128)(2,1)})) %all-reduce.17.cloned.1.call-update) | async-done | bytes 1048592 | tf_op jit(solution)/shard_map/psum | solution.py:9
  631.5 5.4 scatter_fusion.1
  636.9 2.2 fusion.5
  639.1 2.0 fusion.11
  641.1 2.2 fusion.1
  643.4 0.2 all-reduce.15.cloned.1.call-start
  643.6 0.3 all-reduce.15.cloned.1.call-update
  644.0 110.1 %all-reduce.13.cloned.1.call-done = bf16[1024,256]{0,1:T(8,128)(2,1)} async-done(((bf16[1024,256]{0,1:T(8,128)(2,1)}), bf16[1024,256]{0,1:T(8,128)(2,1)}) %all-reduce.13.cloned.1.call-update) | async-done | bytes 524304 | tf_op jit(solution)/shard_map/psum | solution.py:9
  754.1 164.3 %all-reduce.15.cloned.1.call-done = bf16[256,1024]{1,0:T(8,128)(2,1)} async-done(((bf16[256,1024]{1,0:T(8,128)(2,1)}), bf16[256,1024]{1,0:T(8,128)(2,1)}) %all-reduce.15.cloned.1.call-update) | async-done | bytes 524304 | tf_op jit(solution)/shard_map/psum | solution.py:9
  918.5 3.7 and_select_fusion.1
  922.5 1.8 select_select_fusion
  924.5 1.3 fusion.7
  925.8 2.8 reshape.658
  (41 shorter events, 1.2 us)
Async XLA Ops:
  6.5 172.7 %all-reduce.19.cloned.1.call-start = ((), (), s32[]{:S(2)}) async-start(), calls=%async_computation.5 | async-start | bytes 2097152 | tf_op jit(solution)/shard_map/psum | solution.py:9
  14.5 281.3 %all-reduce.9.cloned.1.call-start = ((), (), s32[]{:S(2)}) async-start(), calls=%async_computation | async-start | bytes 1048576 | tf_op jit(solution)/shard_map/psum | solution.py:9
  179.2 3.4 copy-start.1
  179.2 3.4 copy-start.4
  182.5 1.4 copy-start.5
  185.0 275.2 %all-reduce.11.cloned.1.call-start = ((), (), s32[]{:S(2)}) async-start(), calls=%async_computation.1 | async-start | bytes 1048576 | tf_op jit(solution)/shard_map/psum | solution.py:9
  185.8 445.7 %all-reduce.17.cloned.1.call-start = ((), (), s32[]{:S(2)}) async-start(), calls=%async_computation.4 | async-start | bytes 2097152 | tf_op jit(solution)/shard_map/psum | solution.py:9
  460.3 3.6 copy-start
  460.3 6.5 copy-start.3
  473.4 280.7 %all-reduce.13.cloned.1.call-start = ((), (), s32[]{:S(2)}) async-start(), calls=%async_computation.2 | async-start | bytes 1048576 | tf_op jit(solution)/shard_map/psum | solution.py:9
  631.5 5.4 copy-start.2
  643.4 275.1 %all-reduce.15.cloned.1.call-start = ((), (), s32[]{:S(2)}) async-start(), calls=%async_computation.3 | async-start | bytes 1048576 | tf_op jit(solution)/shard_map/psum | solution.py:9
Sparse Core Ops, SparseCore 0:
  14.6 164.5 all-reduce.18
  185.2 110.5 all-reduce.8
  299.5 160.6 all-reduce.10
  473.6 157.9 all-reduce.16
  643.5 110.5 all-reduce.12
  757.7 160.6 all-reduce.14
where the time goes:
time: 936 us; the launch traced here: 935 us
  waiting for transfers between devices  872 us (93%)
  local copies, waits for them, and re-layouts  20.3 us (2%)
  other arithmetic  15.3 us (2%)
  matrix products  13.9 us (1%)
  between operations  13.7 us (1%)
    psum x6, waiting for transfers between devices, spread(): return lax.psum(block, axis)  871 us
  transfers between devices with their start and end apart: 6, of which 6 were waited for; matrix products, arithmetic and copies ran while one was open for 0% of the time, Pallas kernels for 0%

commit v1 on v0

--- a/solution.py
+++ b/solution.py
@@ -6,7 +6,7 @@
 
 def spread(block, axis, source):
     block = jnp.where(lax.axis_index(axis) == source, block, jnp.zeros_like(block))
-    return lax.psum(block, axis)
+    return jnp.sum(lax.all_gather(block, axis), axis=0)
 
 
 def local(matrix, pivots, lower_inverse, upper_inverse):

time: 936 us -> 1120 us (1.20)
  the two profiles are of different devices: /device:TPU:64 before, /device:TPU:8 now
where the time goes in v1:
time: 1120 us
  waiting for transfers between devices  995 us (89%)
  other arithmetic  56.4 us (5%)
  local copies, waits for them, and re-layouts  40.8 us (4%)
  between operations  13.8 us (1%)
  matrix products  12.5 us (1%)
    all_gather x6, waiting for transfers between devices, spread(): return jnp.sum(lax.all_gather(block, axis), axis=0)  701 us
    psum x2, waiting for transfers between devices, local(): incoming = lax.psum(picked, 'prow').astype(jnp.float32)  294 us
    reduce_sum x6, other arithmetic, spread(): return jnp.sum(lax.all_gather(block, axis), axis=0)  44 us
    unnamed x19, local copies, waits for them, and re-layouts  22.6 us
  transfers between devices with their start and end apart: 8, of which 8 were waited for; matrix products, arithmetic and copies ran while one was open for 4% of the time, Pallas kernels for 0%

profile of v1, /device:TPU:8, one launch (start us, length us, event | category | flops | bytes accessed | tf_op | source)
XLA Modules:
  0.0 1119.4 jit_solution(15600051954794063893)
XLA Ops:
  6.5 1.3 slice_select_fusion.4
  7.8 1.2 select_n.396
  9.0 2.1 copy.7
  11.2 1.2 gather_fusion
  13.4 146.0 %all-gather.12.cloned.1.call-done = bf16[32,256,1024]{2,1,0:T(8,128)(2,1)} async-done(((bf16[1,256,1024]{2,1,0:T(8,128)(2,1)}), bf16[32,256,1024]{2,1,0:T(8,128)(2,1)}) %all-gather.12.cloned.1.call-update) | async-done | bytes 16777232 | tf_op jit(solution)/shard_map/all_gather | solution.py:9
  159.4 9.1 reduce_sum.72
  168.5 2.8 scatter_fusion
  171.4 147.7 %all-reduce.3.cloned.1.call-done = bf16[256,1024]{1,0:T(8,128)(2,1)} async-done(((bf16[256,1024]{1,0:T(8,128)(2,1)}), bf16[256,1024]{1,0:T(8,128)(2,1)}) %all-reduce.3.cloned.1.call-update) | async-done | bytes 524304 | tf_op jit(solution)/shard_map/psum | solution.py:37
  319.1 1.2 fusion.2
  323.0 56.4 %all-gather.14.cloned.1.call-done = bf16[16384,256]{1,0:T(8,128)(2,1)} async-done(((bf16[1024,256]{1,0:T(8,128)(2,1)}), bf16[16384,256]{1,0:T(8,128)(2,1)}) %all-gather.14.cloned.1.call-update) | async-done | bytes 8388624 | tf_op jit(solution)/shard_map/all_gather | solution.py:9
  379.4 4.8 reduce_sum.73
  384.2 152.2 %all-gather.16.cloned.1.call-done = bf16[8192,1024]{0,1:T(8,128)(2,1)} async-done(((bf16[256,1024]{0,1:T(8,128)(2,1)}), bf16[8192,1024]{0,1:T(8,128)(2,1)}) %all-gather.16.cloned.1.call-update) | async-done | bytes 16777232 | tf_op jit(solution)/shard_map/all_gather | solution.py:9
  536.4 10.3 copy.8
  546.7 8.1 bitcast_reduce_fusion.1
  555.8 2.3 and_select_fusion
  558.1 2.8 fusion.6
  560.9 2.2 broadcast_select_fusion.2
  563.5 3.4 gather_fusion.1
  567.9 137.0 %all-gather.18.cloned.1.call-done = bf16[8192,1024]{1,0:T(8,128)(2,1)} async-done(((bf16[256,1024]{1,0:T(8,128)(2,1)}), bf16[8192,1024]{1,0:T(8,128)(2,1)}) %all-gather.18.cloned.1.call-update) | async-done | bytes 16777232 | tf_op jit(solution)/shard_map/all_gather | solution.py:9
  705.0 9.1 reduce_sum.75
  714.0 4.8 scatter_fusion.1
  718.9 145.9 %all-reduce.5.cloned.1.call-done = bf16[256,1024]{1,0:T(8,128)(2,1)} async-done(((bf16[256,1024]{1,0:T(8,128)(2,1)}), bf16[256,1024]{1,0:T(8,128)(2,1)}) %all-reduce.5.cloned.1.call-update) | async-done | bytes 524304 | tf_op jit(solution)/shard_map/psum | solution.py:37
  864.8 2.3 fusion.5
  867.1 2.0 fusion.12
  869.1 2.2 fusion.3
  872.2 56.9 %all-gather.20.cloned.1.call-done = bf16[16384,256]{1,0:T(8,128)(2,1)} async-done(((bf16[1024,256]{1,0:T(8,128)(2,1)}), bf16[16384,256]{1,0:T(8,128)(2,1)}) %all-gather.20.cloned.1.call-update) | async-done | bytes 8388624 | tf_op jit(solution)/shard_map/all_gather | solution.py:9
  929.1 4.8 reduce_sum.76
  933.9 151.9 %all-gather.22.cloned.1.call-done = bf16[8192,1024]{0,1:T(8,128)(2,1)} async-done(((bf16[256,1024]{0,1:T(8,128)(2,1)}), bf16[8192,1024]{0,1:T(8,128)(2,1)}) %all-gather.22.cloned.1.call-update) | async-done | bytes 16777232 | tf_op jit(solution)/shard_map/all_gather | solution.py:9
  1085.8 10.3 copy.9
  1096.1 8.1 bitcast_reduce_fusion
  1105.2 3.4 and_select_fusion.1
  1109.8 2.8 reshape.668
  (59 shorter events, 9.1 us)
Async XLA Ops:
  6.5 152.9 %all-gather.12.cloned.1.call-start = ((), (), s32[]{:S(2)}) async-start(), calls=%async_computation | async-start | bytes 17301504 | tf_op jit(solution)/shard_map/all_gather | solution.py:9
  9.0 310.1 %all-reduce.3.cloned.1.call-start = ((), (), s32[]{:S(2)}) async-start(), calls=%async_computation.1 | async-start | bytes 1048576 | tf_op jit(solution)/shard_map/psum | solution.py:37
  9.0 2.1 copy-start.4
  13.3 366.1 %all-gather.14.cloned.1.call-start = ((), (), s32[]{:S(2)}) async-start(), calls=%async_computation.3 | async-start | bytes 8912896 | tf_op jit(solution)/shard_map/all_gather | solution.py:9
  168.5 150.5 %copy-start.5 = (bf16[2,256,256]{2,1,0:T(8,128)(2,1)S(1)}, bf16[2,256,256]{2,1,0:T(8,128)(2,1)}, u32[]{:S(2)}) copy-start(bf16[2,256,256]{2,1,0:T(8,128)(2,1)} %param.18) | copy-start | bytes 786436
  171.4 149.1 %copy-start.6 = (bf16[2,256,256]{2,1,0:T(8,128)(2,1)S(1)}, bf16[2,256,256]{2,1,0:T(8,128)(2,1)}, u32[]{:S(2)}) copy-start(bf16[2,256,256]{2,1,0:T(8,128)(2,1)} %param.19) | copy-start | bytes 786436
  319.1 1.2 copy-start.2
  321.6 214.8 %all-gather.16.cloned.1.call-start = ((), (), s32[]{:S(2)}) async-start(), calls=%async_computation.4 | async-start | bytes 17301504 | tf_op jit(solution)/shard_map/all_gather | solution.py:9
  322.2 382.7 %all-gather.18.cloned.1.call-start = ((), (), s32[]{:S(2)}) async-start(), calls=%async_computation.5 | async-start | bytes 17301504 | tf_op jit(solution)/shard_map/all_gather | solution.py:9
  555.8 5.1 copy-start
  563.2 301.6 %all-reduce.5.cloned.1.call-start = ((), (), s32[]{:S(2)}) async-start(), calls=%async_computation.2 | async-start | bytes 1048576 | tf_op jit(solution)/shard_map/psum | solution.py:37
  567.9 361.2 %all-gather.20.cloned.1.call-start = ((), (), s32[]{:S(2)}) async-start(), calls=%async_computation.6 | async-start | bytes 8912896 | tf_op jit(solution)/shard_map/all_gather | solution.py:9
  718.9 150.3 %copy-start.7 = (bf16[2,256,256]{2,1,0:T(8,128)(2,1)S(1)}, bf16[2,256,256]{2,1,0:T(8,128)(2,1)}, u32[]{:S(2)}) copy-start(bf16[2,256,256]{2,1,0:T(8,128)(2,1)} %param.19) | copy-start | bytes 786436
  864.8 2.3 copy-start.3
  871.3 214.5 %all-gather.22.cloned.1.call-start = ((), (), s32[]{:S(2)}) async-start(), calls=%async_computation.7 | async-start | bytes 17301504 | tf_op jit(solution)/shard_map/all_gather | solution.py:9
  1105.2 4.4 copy-start.1
Sparse Core Ops, SparseCore 0:
  10.5 148.8 all-gather.11
  162.8 156.1 all-reduce.2
  321.8 57.5 all-gather.13
  382.7 153.6 all-gather.15
  563.3 141.5 all-gather.17
  708.6 156.1 all-reduce.4
  871.5 57.5 all-gather.19
  932.1 153.6 all-gather.21
